TPU v7x, 32 devices: a whole 2x2x4 slice. The times are simulated.
32 devices in a mesh: net: 2 (over y), obs: 4 (over z), state: 4 (over x, core).
Axes of the slice: x: 2, y: 2, z: 4, core: 2. Of those that a mesh axis runs over, the one named last changes fastest.
Arguments:
- anomalies: bfloat16 [4, 512, 512], P('state', 'obs'), may hold values from -6 to 6
- prior_ensemble_mean: float32 [4, 512], P('state', 'obs'), may hold values from -6 to 6
- operator_blocks: bfloat16 [64, 4, 8, 128, 128], P(('net', 'obs'), 'state'), parts along dimension 0, may hold values from -0.09375 to 0.09375
- block_column_ids: int32 [64, 4, 8], P(('net', 'obs'), 'state'), parts along dimension 0, may hold values from 0 to 3
- observation_counts: int32 [64], P(('net', 'obs')), parts along dimension 0, may hold values from 1 to 128, as said below
- observed_readings: float32 [64, 128], P(('net', 'obs')), parts along dimension 0, may hold values from -6 to 6
- observation_error_std: float32 [64, 128], P(('net', 'obs')), parts along dimension 0, may hold values from 0.25 to 4
Outputs:
- analysis: bfloat16 [8, 512, 512], P(('net', 'state'), 'obs'), parts along dimension 0
There are 2 independent parts, one for each index of `net`. A program takes and returns all parts, laid end to end along the dimension named above; an argument that names none is the same for every part. Nothing has to cross between parts.
Inputs may be any that keep to these rules, and one draw needn't show every extreme that they name: `observation_counts`: some observation block of every network is full.
All inputs are finite; a program needn't handle non-finite values.
Results may differ from a plain program's by a relative error of at most 0.0053.
Values may be sent and summed in bfloat16 or wider, within the bound.
A program may use at most 64 MiB of HBM per device.

v0:
```python
import jax
import jax.numpy as jnp
from jax import lax
from jax.sharding import PartitionSpec as P


def local(
    anomalies,
    prior_ensemble_mean,
    operator_blocks,
    block_column_ids,
    observation_counts,
    observed_readings,
    observation_error_std,
):
    members = anomalies.shape[2]
    blk = operator_blocks.shape[3]
    local_cells = anomalies[0]
    slab_local_mean = prior_ensemble_mean[0]
    slab_anom, slab_mean = (
        lax.all_gather(local_cells, "obs", axis=0, tiled=True),
        lax.all_gather(slab_local_mean.astype(jnp.bfloat16), "obs", axis=0, tiled=True),
    )
    nblocks = slab_anom.shape[0] // blk
    cells = slab_anom.reshape(nblocks, blk, members)
    mean_blocks = slab_mean.reshape(nblocks, blk)

    def one_block(inputs):
        values, columns = inputs
        picked = cells[columns]
        picked_mean = mean_blocks[columns]
        rows_anom = jnp.einsum("jrc,jck->rk", values, picked, preferred_element_type=jnp.float32)
        rows_mean = jnp.einsum("jrc,jc->r", values, picked_mean, preferred_element_type=jnp.float32)
        return (rows_anom, rows_mean)

    part_anom, part_mean = lax.map(one_block, (operator_blocks[:, 0], block_column_ids[:, 0]))
    nrows = part_anom.shape[0] * blk
    part_anom = part_anom.reshape(nrows, members)
    part_mean = part_mean.reshape(nrows)
    valid = (jnp.arange(blk, dtype=jnp.int32)[None, :] < observation_counts[:, None]).astype(
        jnp.float32
    )
    weight_all = (valid / observation_error_std).reshape(nrows)
    observed_all = observed_readings.reshape(nrows)
    obs_anom, obs_mean = lax.psum((part_anom, part_mean), "state")
    scaled = obs_anom * weight_all[:, None]
    innovation = weight_all * (observed_all - obs_mean)
    gram_part = jnp.dot(scaled.T, scaled, precision=lax.Precision.HIGHEST)
    rhs_part = jnp.dot(scaled.T, innovation[:, None], precision=lax.Precision.HIGHEST)
    gram, rhs = lax.psum((gram_part, rhs_part), "obs")
    identity = jnp.eye(members, dtype=jnp.float32)
    gram = gram + (members - 1.0) * identity
    lower = jnp.linalg.cholesky(gram)
    middle = lax.linalg.triangular_solve(lower, rhs, left_side=True, lower=True)
    mean_weights = lax.linalg.triangular_solve(
        lower, middle, left_side=True, lower=True, transpose_a=True
    )
    transform = jnp.sqrt(members - 1.0) * lax.linalg.triangular_solve(
        lower, identity, left_side=True, lower=True, transpose_a=True
    )
    mixing = (transform + mean_weights).astype(jnp.bfloat16)
    shifted_values = jnp.dot(local_cells, mixing, preferred_element_type=jnp.float32)
    analysis_output = (slab_local_mean[:, None] + shifted_values).astype(jnp.bfloat16)
    return analysis_output[None]


def solution(mesh):
    placed = (
        P("state", "obs", None),
        P("state", "obs"),
        P(("net", "obs"), "state", None, None, None),
        P(("net", "obs"), "state", None),
        P(("net", "obs")),
        P(("net", "obs"), None),
        P(("net", "obs"), None),
    )
    return jax.shard_map(
        local,
        mesh=mesh,
        in_specs=placed,
        out_specs=P(("net", "state"), "obs", None),
        check_vma=False,
    )
```

profile of v0, /device:TPU:0, one launch (start us, length us, event | category | flops | bytes accessed | tf_op | source)
XLA Modules:
  0.0 340.0 jit_solution(5647451602171519682)
XLA Ops:
  6.5 17.6 %all-gather = bf16[1,512,512]{2,1,0:T(8,128)(2,1)S(1)} all-gather(bf16[1,128,512]{2,1,0:T(8,128)(2,1)} %param.9), channel_id=2, replica_groups=mesh['net'=2,'obs'=4,'state'=4] {'obs'}, dimensions={1}, use_global_device_ids=true | all-gather | bytes 655360 | tf_op jit(solution)/shard_map/all_gather | solution.py:21
  24.8 11.6 %all-gather.1 = bf16[4,1,128]{2,1,0:T(2,128)(2,1)S(1)} all-gather(bf16[1,1,128]{2,1,0:T(2,128)(2,1)S(1)} %convert_bitcast_fusion), channel_id=1, replica_groups=mesh['net'=2,'obs'=4,'state'=4] {'obs'}, dimensions={0}, use_global_device_ids=true | all-gather | bytes 1280 | tf_op jit(solution)/shard_map/all_gather | solution.py:22
  36.4 40.2 %while.13 = (s32[]{:T(128)}, f32[8,128,512]{2,1,0:T(8,128)}, f32[8,128]{1,0:T(8,128)S(1)}, bf16[8,8,128,128]{3,2,1,0:T(8,128)(2,1)}, s32[8,8]{1,0:T(8,128)}, /*i...) while((s32[]{:T(128)}, f32[8,128,512]{2,1,0:T(8,128)}, ...), condition=%wide.region_1.2_spmd, body=%wide.region_0.1_spmd.sunk | while | flops 134480928 | bytes 3945733 | solution.py:36
  39.4 2.0 fusion.127
  44.5 2.0 fusion.127
  49.5 2.0 fusion.127
  54.5 2.0 fusion.127
  59.5 2.0 fusion.127
  64.6 2.0 fusion.127
  74.6 2.0 fusion.127
  76.7 5.7 %psum.30 = f32[1024]{0:T(1024)S(1)} all-reduce(f32[1024]{0:T(1024)S(1)} %bitcast.218), channel_id=1, replica_groups=mesh['net'=2,'obs'=4,'state'=4] {'state'}, use_global_device_ids=true, to_apply=%region_12.13 | all-reduce | flops 1024 | bytes 8192 | tf_op jit(solution)/shard_map/psum | solution.py:45
  82.4 43.9 %all-reduce.4.cloned.1.call-done = f32[1024,512]{1,0:T(8,128)} async-done(((f32[1024,512]{1,0:T(8,128)}), f32[1024,512]{1,0:T(8,128)}) %all-reduce.4.cloned.1.call-update) | async-done | bytes 2097168 | tf_op jit(solution)/shard_map/psum | solution.py:45
  126.4 7.5 %fusion.12 = f32[512,512]{0,1:T(8,128)} fusion(f32[1024,512]{1,0:T(8,128)} %all-reduce.4.cloned.1.call-done, f32[1024]{0:T(1024)S(1)} %get-tuple-element.88), kind=kOutput, calls=%fused_computation.21 | convolution fusion | flops 3221749760 | bytes 3149824 | tf_op jit(solution)/shard_map/dot_general | solution.py:48
  136.5 12.2 %psum.31 = f32[512,1]{0,1:T(1,128)S(1)} all-reduce(f32[512,1]{0,1:T(1,128)S(1)} %fusion.16), channel_id=1, replica_groups=mesh['net'=2,'obs'=4,'state'=4] {'obs'}, use_global_device_ids=true, to_apply=%region_13.14 | all-reduce | flops 512 | bytes 4096 | tf_op jit(solution)/shard_map/psum | solution.py:50
  148.6 37.6 %all-reduce.6.cloned.1.call-done = f32[512,512]{0,1:T(8,128)} async-done(((f32[512,512]{0,1:T(8,128)}), f32[512,512]{0,1:T(8,128)}) %all-reduce.6.cloned.1.call-update) | async-done | bytes 1048592 | tf_op jit(solution)/shard_map/psum | solution.py:50
  188.2 11.7 %cholesky.103 = f32[128,128]{1,0:T(8,128)S(1)} custom-call(f32[128,128]{1,0:T(8,128)S(1)} %cholesky.263), custom_call_target="Cholesky" | custom-call | tf_op jit(solution)/shard_map/jit(cholesky)/cholesky | solution.py:53
  200.0 9.8 %custom-call.34 = f32[1,128,128]{1,2,0:T(8,128)S(1)} custom-call(f32[1,128,128]{2,1,0:T(8,128)S(1)} %get-tuple-element.96), custom_call_target="InvertDiagBlocksLowerTriangular" | custom-call | tf_op jit(solution)/shard_map/jit(cholesky)/cholesky | solution.py:53
  210.4 11.7 %cholesky.215 = f32[128,128]{1,0:T(8,128)S(1)} custom-call(f32[128,128]{1,0:T(8,128)S(1)} %cholesky.267), custom_call_target="Cholesky" | custom-call | tf_op jit(solution)/shard_map/jit(cholesky)/cholesky | solution.py:53
  222.5 10.0 %custom-call.35 = f32[1,128,128]{1,2,0:T(8,128)S(1)} custom-call(f32[1,128,128]{2,1,0:T(8,128)S(1)} %get-tuple-element.94), custom_call_target="InvertDiagBlocksLowerTriangular" | custom-call | tf_op jit(solution)/shard_map/jit(cholesky)/cholesky | solution.py:53
  233.6 11.7 %cholesky.236 = f32[128,128]{1,0:T(8,128)S(1)} custom-call(f32[128,128]{1,0:T(8,128)S(1)} %cholesky.272), custom_call_target="Cholesky" | custom-call | tf_op jit(solution)/shard_map/jit(cholesky)/cholesky | solution.py:53
  245.5 9.8 %custom-call.36 = f32[1,128,128]{1,2,0:T(8,128)S(1)} custom-call(f32[1,128,128]{2,1,0:T(8,128)S(1)} %get-tuple-element.92), custom_call_target="InvertDiagBlocksLowerTriangular" | custom-call | tf_op jit(solution)/shard_map/jit(cholesky)/cholesky | solution.py:53
  256.1 11.9 %cholesky.253 = f32[128,128]{1,0:T(8,128)S(1)} custom-call(f32[128,128]{1,0:T(8,128)S(1)} %convolution_subtract_fusion.5), custom_call_target="Cholesky" | custom-call | tf_op jit(solution)/shard_map/jit(cholesky)/cholesky | solution.py:53
  272.9 11.0 %while.14 = (s32[]{:T(128)}, f32[512,512]{0,1:T(8,128)S(1)}, s32[4,2]{0,1:T(2,128)S(1)}, f32[4,128,128]{2,1,0:T(8,128)}, s32[]{:T(128)}) while((s32[]{:T(128)}, f32[512,512]{0,1:T(8,128)S(1)}, s32[4,2]{0,1:T(2,128)S(1)}, f32[4,128,128]{2,1,0:T(8,128)}, s32[]{:T(128)}) %tuple.43), condition=%wide.while_cond, body=%wide.while_body.sunk | while | flops 2 | bytes 393829 | solution.py:58
  283.8 40.1 %custom-call.37 = f32[4,128,128]{1,2,0:T(8,128)S(1)} custom-call(f32[4,128,128]{2,1,0:T(8,128)} %get-tuple-element.52), custom_call_target="InvertDiagBlocksLowerTriangular" | custom-call | tf_op jit(solution)/shard_map/triangular_solve | solution.py:58
  (154 shorter events, 56.4 us)
Async XLA Ops:
  6.5 119.9 %all-reduce.4.cloned.1.call-start = ((), (), s32[]{:S(2)}) async-start(), calls=%async_computation | async-start | bytes 4194304 | tf_op jit(solution)/shard_map/psum | solution.py:45
  76.6 5.8 %copy-start.4 = (f32[8,128]{1,0:T(8,128)S(1)}, f32[8,128]{1,0:T(8,128)}, u32[]{:S(2)}) copy-start(f32[8,128]{1,0:T(8,128)} %param.14) | copy-start | bytes 12292
  76.6 5.8 %copy-start.5 = (f32[8,128]{1,0:T(8,128)S(1)}, f32[8,128]{1,0:T(8,128)}, u32[]{:S(2)}) copy-start(f32[8,128]{1,0:T(8,128)} %param.15) | copy-start | bytes 12292
  76.6 5.8 %copy-start.6 = (s32[8]{0:T(128)S(1)}, s32[8]{0:T(128)}, u32[]{:S(2)}) copy-start(s32[8]{0:T(128)} %param.13) | copy-start | bytes 100
  76.6 109.6 %all-reduce.6.cloned.1.call-start = ((), (), s32[]{:S(2)}) async-start(), calls=%async_computation.1 | async-start | bytes 2097152 | tf_op jit(solution)/shard_map/psum | solution.py:50
  126.4 8.8 %copy-start.2 = (f32[1024,512]{1,0:T(8,128)S(1)}, f32[1024,512]{1,0:T(8,128)}, u32[]{:S(2)}) copy-start(f32[1024,512]{1,0:T(8,128)} %all-reduce.4.cloned.1.call-done) | copy-start | bytes 6291460
  186.2 1.8 copy-start
  272.9 54.4 %copy-start.1 = (f32[512,512]{0,1:T(8,128)S(1)}, f32[512,512]{0,1:T(8,128)}, u32[]{:S(2)}) copy-start(f32[512,512]{0,1:T(8,128)} %fusion.38) | copy-start | bytes 3145732
  327.8 3.6 %copy-start.3 = (bf16[1,128,512]{2,1,0:T(8,128)(2,1)S(1)}, bf16[1,128,512]{2,1,0:T(8,128)(2,1)}, u32[]{:S(2)}) copy-start(bf16[1,128,512]{2,1,0:T(8,128)(2,1)} %param.9) | copy-start | bytes 393220
  327.9 3.6 %copy-start.7 = (f32[1,128]{1,0:T(1,128)S(1)}, f32[1,128]{1,0:T(1,128)}, u32[]{:S(2)}) copy-start(f32[1,128]{1,0:T(1,128)} %param.10) | copy-start | bytes 1540
Sparse Core Ops, SparseCore 0:
  76.8 49.5 all-reduce.3
  134.1 52.0 all-reduce.5
where the time goes:
time: 346 us; the launch traced here: 340 us
  other arithmetic  128 us (37%)
  waiting for transfers between devices  81.5 us (24%)
  blocking collectives  47 us (14%)
  matrix products  43.8 us (13%)
  local copies, waits for them, and re-layouts  22.5 us (7%)
  between operations  16.7 us (5%)
    another operation x14, other arithmetic, local(): lower = jnp.linalg.cholesky(gram)  78.8 us
    psum x1, waiting for transfers between devices, local(): obs_anom, obs_mean = lax.psum((part_anom, part_mean), 'state')  43.9 us
    another operation x3, other arithmetic, local(): lax.linalg.triangular_solve(lower, identity, left_side=True, lower=True,...  40.3 us
    psum x1, waiting for transfers between devices, local(): gram, rhs = lax.psum((gram_part, rhs_part), 'obs')  37.6 us
    all_gather x1, blocking collectives, local(): lax.all_gather(local_cells, 'obs', axis=0, tiled=True)  17.6 us
    dot_general x8, matrix products, one_block(): jnp.einsum('jrc,jck->rk', values, picked, preferred_element_type=jnp.floa...  15.8 us
    psum x1, blocking collectives, local(): gram, rhs = lax.psum((gram_part, rhs_part), 'obs')  12.2 us
    all_gather x1, blocking collectives, local(): lax.all_gather(slab_local_mean.astype(jnp.bfloat16), 'obs', axis=0, tiled...  11.6 us
  transfers between devices with their start and end apart: 2, of which 2 were waited for; matrix products, arithmetic and copies ran while one was open for 1% of the time, Pallas kernels for 0%

commit v1 on v0

--- a/solution.py
+++ b/solution.py
@@ -1,7 +1,83 @@
+import functools
 import jax
 import jax.numpy as jnp
 from jax import lax
+from jax.experimental import pallas as pl
+from jax.experimental.pallas import tpu as pltpu
 from jax.sharding import PartitionSpec as P
+
+BLK = 128
+HI = lax.Precision.HIGHEST
+NT = (((1,), (1,)), ((), ()))
+
+
+def inverse_factor(block):
+    row = lax.broadcasted_iota(jnp.int32, (BLK, BLK), 0)
+    col = lax.broadcasted_iota(jnp.int32, (BLK, BLK), 1)
+    eye = (row == col).astype(jnp.float32)
+    groups = BLK // 8
+    left = [block[8 * g : 8 * g + 8] for g in range(groups)]
+    right = [eye[8 * g : 8 * g + 8] for g in range(groups)]
+    sub = lax.broadcasted_iota(jnp.int32, (8, 1), 0)
+    for k in range(BLK - 1):
+        g, i = divmod(k, 8)
+        lrow = left[g][i : i + 1, :]
+        rrow = right[g][i : i + 1, :]
+        inv = 1.0 / lrow[:, k : k + 1]
+        lrow = lrow * inv
+        rrow = rrow * inv
+        for h in range(g, groups):
+            c = left[h][:, k : k + 1]
+            if h == g:
+                if i == 7:
+                    continue
+                c = jnp.where(sub > i, c, 0.0)
+            left[h] = left[h] - c * lrow
+            right[h] = right[h] - c * rrow
+    full = jnp.concatenate(left, axis=0)
+    diag = jnp.sum(jnp.where(row == col, full, 0.0), axis=1, keepdims=True)
+    return jnp.concatenate(right, axis=0) * lax.rsqrt(diag)
+
+
+def finish_kernel(gram_ref, rhs_ref, anom_ref, mean_ref, out_ref, work):
+    members = gram_ref.shape[1]
+    cells = anom_ref.shape[0]
+    total = members + cells + 8
+    work[0:members, :] = gram_ref[...]
+    work[members : members + cells, :] = anom_ref[...].astype(jnp.float32)
+    work[members + cells : total, :] = rhs_ref[...]
+
+    @pl.loop(0, members // BLK)
+    def _(p):
+        off = pl.multiple_of(p * BLK, BLK)
+        inv = inverse_factor(work[pl.ds(off, BLK), pl.ds(off, BLK)])
+        x = lax.dot_general(
+            work[:, pl.ds(off, BLK)], inv, NT, precision=HI, preferred_element_type=jnp.float32
+        )
+        rows = lax.broadcasted_iota(jnp.int32, (total, 1), 0)
+        x = jnp.where(rows >= off + BLK, x, 0.0)
+        work[...] -= lax.dot_general(
+            x, x[:members], NT, precision=HI, preferred_element_type=jnp.float32
+        )
+        work[members:total, pl.ds(off, BLK)] = x[members:]
+
+    solved = work[members : members + cells, :]
+    shift = jnp.sum(solved * work[members + cells : members + cells + 1, :], axis=1, keepdims=True)
+    root = (members - 1.0) ** 0.5
+    out_ref[...] = (mean_ref[...] + (root * solved + shift)).astype(jnp.bfloat16)
+
+
+def finish(gram, rhs_rows, cells, mean_col):
+    members = gram.shape[1]
+    ncells = cells.shape[0]
+    return pl.pallas_call(
+        finish_kernel,
+        out_shape=jax.ShapeDtypeStruct((ncells, members), jnp.bfloat16),
+        in_specs=[pl.BlockSpec(memory_space=pltpu.VMEM)] * 4,
+        out_specs=pl.BlockSpec(memory_space=pltpu.VMEM),
+        scratch_shapes=[pltpu.VMEM((members + ncells + 8, members), jnp.float32)],
+        compiler_params=pltpu.CompilerParams(vmem_limit_bytes=32 << 20),
+    )(gram, rhs_rows, cells, mean_col)
 
 
 def local(
@@ -50,18 +126,9 @@
     gram, rhs = lax.psum((gram_part, rhs_part), "obs")
     identity = jnp.eye(members, dtype=jnp.float32)
     gram = gram + (members - 1.0) * identity
-    lower = jnp.linalg.cholesky(gram)
-    middle = lax.linalg.triangular_solve(lower, rhs, left_side=True, lower=True)
-    mean_weights = lax.linalg.triangular_solve(
-        lower, middle, left_side=True, lower=True, transpose_a=True
-    )
-    transform = jnp.sqrt(members - 1.0) * lax.linalg.triangular_solve(
-        lower, identity, left_side=True, lower=True, transpose_a=True
-    )
-    mixing = (transform + mean_weights).astype(jnp.bfloat16)
-    shifted_values = jnp.dot(local_cells, mixing, preferred_element_type=jnp.float32)
-    analysis_output = (slab_local_mean[:, None] + shifted_values).astype(jnp.bfloat16)
-    return analysis_output[None]
+    rhs_rows = jnp.concatenate([rhs.T, jnp.zeros((7, members), jnp.float32)], axis=0)
+    out = finish(gram, rhs_rows, local_cells, slab_local_mean[:, None])
+    return out[None]
 
 
 def solution(mesh):

time: 346 us -> 246 us (0.71); the launches traced: 340 us -> 245 us
  other arithmetic: 128 us -> 7.69 us
  Pallas kernels: 0 us -> 50.9 us
  local copies, waits for them, and re-layouts: 22.5 us -> 9.87 us
  matrix products: 43.8 us -> 33.5 us
    another operation x18 -> x0, other arithmetic: 119 us -> none  [the longest x14 78.8 us: local(): lower = jnp.linalg.cholesky(gram)]
    pallas_call x0 -> x1, Pallas kernels: none -> 50.9 us  [finish(): pl.pallas_call(finish_kernel, out_shape=jax.ShapeDtypeStruct((ncells, mem...]
    another operation x34 -> x1, local copies, waits for them, and re-layouts: 11.6 us -> 0.11 us  [local(): out = finish(gram, rhs_rows, local_cells, slab_local_mean[:, None])]
    another operation x27 -> x0, matrix products: 9.7 us -> none  [the longest x7 4.47 us: local(): lax.linalg.triangular_solve(lower, identity, left_side=True, lower=True,...]
where the time goes in v1:
time: 246 us; the launch traced here: 245 us
  waiting for transfers between devices  82.8 us (34%)
  Pallas kernels  50.9 us (21%)
  blocking collectives  46.7 us (19%)
  matrix products  33.5 us (14%)
  between operations  13.5 us (5%)
  local copies, waits for them, and re-layouts  9.87 us (4%)
  other arithmetic  7.69 us (3%)
    pallas_call x1, Pallas kernels, finish(): pl.pallas_call(finish_kernel, out_shape=jax.ShapeDtypeStruct((ncells, mem...  50.9 us
    psum x1, waiting for transfers between devices, local(): obs_anom, obs_mean = lax.psum((part_anom, part_mean), 'state')  43.9 us
    psum x1, waiting for transfers between devices, local(): gram, rhs = lax.psum((gram_part, rhs_part), 'obs')  38.8 us
    all_gather x1, blocking collectives, local(): lax.all_gather(local_cells, 'obs', axis=0, tiled=True)  17.6 us
    dot_general x8, matrix products, one_block(): jnp.einsum('jrc,jck->rk', values, picked, preferred_element_type=jnp.floa...  15.8 us
    psum x1, blocking collectives, local(): gram, rhs = lax.psum((gram_part, rhs_part), 'obs')  11.9 us
    all_gather x1, blocking collectives, local(): lax.all_gather(slab_local_mean.astype(jnp.bfloat16), 'obs', axis=0, tiled...  11.6 us
    dot_general x8, matrix products, one_block(): jnp.einsum('jrc,jc->r', values, picked_mean, preferred_element_type=jnp.f...  8.93 us
  transfers between devices with their start and end apart: 2, of which 2 were waited for; matrix products, arithmetic and copies ran while one was open for 1% of the time, Pallas kernels for 0%

profile of v1, /device:TPU:0, one launch (start us, length us, event | category | flops | bytes accessed | tf_op | source)
XLA Modules:
  0.0 245.1 jit_solution(17200519566897762452)
XLA Ops:
  6.5 17.6 %all-gather = bf16[1,512,512]{2,1,0:T(8,128)(2,1)S(1)} all-gather(bf16[1,128,512]{2,1,0:T(8,128)(2,1)} %param.9), channel_id=2, replica_groups=mesh['net'=2,'obs'=4,'state'=4] {'obs'}, dimensions={1}, use_global_device_ids=true | all-gather | bytes 655360 | tf_op jit(solution)/shard_map/all_gather | solution.py:97
  24.8 11.6 %all-gather.1 = bf16[1,512]{1,0:T(2,128)(2,1)S(1)} all-gather(bf16[1,128]{1,0:T(2,128)(2,1)S(1)} %convert_element_type.10), channel_id=3, replica_groups=mesh['net'=2,'obs'=4,'state'=4] {'obs'}, dimensions={1}, use_global_device_ids=true | all-gather | bytes 1280 | tf_op jit(solution)/shard_map/all_gather | solution.py:98
  36.4 40.3 %while.12 = (s32[]{:T(128)}, f32[8,128,512]{2,1,0:T(8,128)}, f32[8,128]{1,0:T(8,128)S(1)}, bf16[8,8,128,128]{3,2,1,0:T(8,128)(2,1)}, s32[8,8]{1,0:T(8,128)}, /*i...) while((s32[]{:T(128)}, f32[8,128,512]{2,1,0:T(8,128)}, ...), condition=%wide.region_1.2_spmd, body=%wide.region_0.1_spmd.sunk | while | flops 134480928 | bytes 3945733 | solution.py:112
  39.4 2.0 fusion.30
  44.5 2.0 fusion.30
  47.7 1.1 convolution_bitcast_fusion.3
  49.5 2.0 fusion.30
  52.7 1.1 convolution_bitcast_fusion.3
  54.5 2.0 fusion.30
  57.8 1.1 convolution_bitcast_fusion.3
  59.6 2.0 fusion.30
  62.8 1.1 convolution_bitcast_fusion.3
  64.6 2.0 fusion.30
  67.9 1.1 convolution_bitcast_fusion.3
  69.6 2.0 fusion.30
  74.7 2.0 fusion.30
  76.7 5.7 %psum.30 = f32[1024]{0:T(1024)S(1)} all-reduce(f32[1024]{0:T(1024)S(1)} %bitcast.66), channel_id=1, replica_groups=mesh['net'=2,'obs'=4,'state'=4] {'state'}, use_global_device_ids=true, to_apply=%region_4.5 | all-reduce | flops 1024 | bytes 8192 | tf_op jit(solution)/shard_map/psum | solution.py:121
  82.5 43.9 %all-reduce.4.cloned.1.call-done = f32[1024,512]{1,0:T(8,128)} async-done(((f32[1024,512]{1,0:T(8,128)}), f32[1024,512]{1,0:T(8,128)}) %all-reduce.4.cloned.1.call-update) | async-done | bytes 2097168 | tf_op jit(solution)/shard_map/psum | solution.py:121
  126.4 7.4 %fusion.12 = f32[512,512]{1,0:T(8,128)} fusion(f32[1024,512]{1,0:T(8,128)} %all-reduce.4.cloned.1.call-done, f32[1024]{0:T(1024)S(1)} %get-tuple-element.60), kind=kOutput, calls=%fused_computation.19 | convolution fusion | flops 3221749760 | bytes 3149824 | tf_op jit(solution)/shard_map/dot_general | solution.py:124
  134.0 1.3 fusion.10
  135.3 11.9 %psum.31 = f32[1,512]{1,0:T(1,128)S(1)} all-reduce(f32[1,512]{1,0:T(1,128)S(1)} %fusion.10), channel_id=1, replica_groups=mesh['net'=2,'obs'=4,'state'=4] {'obs'}, use_global_device_ids=true, to_apply=%region_5.6 | all-reduce | flops 512 | bytes 4096 | tf_op jit(solution)/shard_map/psum | solution.py:126
  147.2 38.8 %all-reduce.6.cloned.1.call-done = f32[512,512]{1,0:T(8,128)} async-done(((f32[512,512]{1,0:T(8,128)}), f32[512,512]{1,0:T(8,128)}) %all-reduce.6.cloned.1.call-update) | async-done | bytes 1048592 | tf_op jit(solution)/shard_map/psum | solution.py:126
  186.0 1.3 select_add_fusion.gram_ref
  187.4 50.9 %shard_map.73 = bf16[128,512]{1,0:T(8,128)(2,1)} custom-call(f32[512,512]{1,0:T(8,128)S(1)} %select_add_fusion.gram_ref, f32[8,512]{1,0:T(8,128)S(1)} %concatenate.3.rhs_ref, bf16[128,512]{1,0:T(8,128)(2,1)S(1)} %bitcast.59, f32[128,1]{1,0:T(8,128)S(1)} %copy.8.mean_ref), custom_call_target="tpu_custom_call" | custom-call | tf_op jit(solution)/shard_map/pallas_call | solution.py:73
  (66 shorter events, 19.7 us)
Async XLA Ops:
  6.5 119.9 %all-reduce.4.cloned.1.call-start = ((), (), s32[]{:S(2)}) async-start(), calls=%async_computation | async-start | bytes 4194304 | tf_op jit(solution)/shard_map/psum | solution.py:121
  76.6 5.8 %copy-start.2 = (f32[8,128]{1,0:T(8,128)S(1)}, f32[8,128]{1,0:T(8,128)}, u32[]{:S(2)}) copy-start(f32[8,128]{1,0:T(8,128)} %param.14) | copy-start | bytes 12292
  76.6 5.8 %copy-start.3 = (f32[8,128]{1,0:T(8,128)S(1)}, f32[8,128]{1,0:T(8,128)}, u32[]{:S(2)}) copy-start(f32[8,128]{1,0:T(8,128)} %param.15) | copy-start | bytes 12292
  76.6 5.8 %copy-start.5 = (s32[8]{0:T(128)S(1)}, s32[8]{0:T(128)}, u32[]{:S(2)}) copy-start(s32[8]{0:T(128)} %param.13) | copy-start | bytes 100
  76.7 109.3 %all-reduce.6.cloned.1.call-start = ((), (), s32[]{:S(2)}) async-start(), calls=%async_computation.1 | async-start | bytes 2097152 | tf_op jit(solution)/shard_map/psum | solution.py:126
  126.4 7.5 %copy-start.4 = (f32[1,128]{1,0:T(1,128)S(1)}, f32[1,128]{1,0:T(1,128)}, u32[]{:S(2)}) copy-start(f32[1,128]{1,0:T(1,128)} %param.10) | copy-start | bytes 1540
  126.4 7.6 %copy-start.1 = (f32[1024,512]{1,0:T(8,128)S(1)}, f32[1024,512]{1,0:T(8,128)}, u32[]{:S(2)}) copy-start(f32[1024,512]{1,0:T(8,128)} %all-reduce.4.cloned.1.call-done) | copy-start | bytes 6291460
  134.0 53.4 %copy-start = (bf16[1,128,512]{2,1,0:T(8,128)(2,1)S(1)}, bf16[1,128,512]{2,1,0:T(8,128)(2,1)}, u32[]{:S(2)}) copy-start(bf16[1,128,512]{2,1,0:T(8,128)(2,1)} %param.9) | copy-start | bytes 393220
Sparse Core Ops, SparseCore 0:
  76.8 49.5 all-reduce.3
  134.0 51.9 all-reduce.5

commit v2 on v1

v2 whole, which is shorter than its diff:
```python
import functools
import jax
import jax.numpy as jnp
from jax import lax
from jax.experimental import pallas as pl
from jax.experimental.pallas import tpu as pltpu
from jax.sharding import PartitionSpec as P

BLK = 128
HI = lax.Precision.HIGHEST
NT = (((1,), (1,)), ((), ()))


def inverse_factor(block):
    row = lax.broadcasted_iota(jnp.int32, (BLK, BLK), 0)
    col = lax.broadcasted_iota(jnp.int32, (BLK, BLK), 1)
    eye = (row == col).astype(jnp.float32)
    groups = BLK // 8
    left = [block[8 * g : 8 * g + 8] for g in range(groups)]
    right = [eye[8 * g : 8 * g + 8] for g in range(groups)]
    sub = lax.broadcasted_iota(jnp.int32, (8, 1), 0)
    for k in range(BLK - 1):
        g, i = divmod(k, 8)
        lrow = left[g][i : i + 1, :]
        rrow = right[g][i : i + 1, :]
        inv = 1.0 / lrow[:, k : k + 1]
        lrow = lrow * inv
        rrow = rrow * inv
        for h in range(g, groups):
            c = left[h][:, k : k + 1]
            if h == g:
                if i == 7:
                    continue
                c = jnp.where(sub > i, c, 0.0)
            left[h] = left[h] - c * lrow
            right[h] = right[h] - c * rrow
    full = jnp.concatenate(left, axis=0)
    diag = jnp.sum(jnp.where(row == col, full, 0.0), axis=1, keepdims=True)
    return jnp.concatenate(right, axis=0) * lax.rsqrt(diag)


def finish_kernel(packed_ref, anom_ref, mean_ref, out_ref, work):
    cells, members = anom_ref.shape
    total = members + cells + 8
    row = lax.broadcasted_iota(jnp.int32, (BLK, BLK), 0)
    col = lax.broadcasted_iota(jnp.int32, (BLK, BLK), 1)
    ridge = jnp.where(row == col, members - 1.0, 0.0)
    start = 0
    for j in range(members // BLK):
        size = members - j * BLK
        cols = slice(j * BLK, (j + 1) * BLK)
        if j:
            work[0 : j * BLK, cols] = jnp.zeros((j * BLK, BLK), jnp.float32)
        work[cols, cols] = packed_ref[start : start + BLK, :] + ridge
        if size > BLK:
            work[(j + 1) * BLK : members, cols] = packed_ref[start + BLK : start + size, :]
        start += size
    for j in range(members // BLK):
        cols = slice(j * BLK, (j + 1) * BLK)
        work[members + cells : total, cols] = jnp.broadcast_to(
            packed_ref[start + j : start + j + 1, :], (8, BLK)
        )
    work[members : members + cells, :] = anom_ref[...].astype(jnp.float32)

    @pl.loop(0, members // BLK)
    def _(p):
        off = pl.multiple_of(p * BLK, BLK)
        inv = inverse_factor(work[pl.ds(off, BLK), pl.ds(off, BLK)])
        x = lax.dot_general(
            work[:, pl.ds(off, BLK)], inv, NT, precision=HI, preferred_element_type=jnp.float32
        )
        rows = lax.broadcasted_iota(jnp.int32, (total, 1), 0)
        x = jnp.where(rows >= off + BLK, x, 0.0)
        work[...] -= lax.dot_general(
            x, x[:members], NT, precision=HI, preferred_element_type=jnp.float32
        )
        work[members:total, pl.ds(off, BLK)] = x[members:]

    solved = work[members : members + cells, :]
    shift = jnp.sum(solved * work[members + cells : members + cells + 1, :], axis=1, keepdims=True)
    root = (members - 1.0) ** 0.5
    out_ref[...] = (mean_ref[...] + (root * solved + shift)).astype(jnp.bfloat16)


def finish(packed, cells, mean_col):
    ncells, members = cells.shape
    return pl.pallas_call(
        finish_kernel,
        out_shape=jax.ShapeDtypeStruct((ncells, members), jnp.bfloat16),
        in_specs=[pl.BlockSpec(memory_space=pltpu.VMEM)] * 3,
        out_specs=pl.BlockSpec(memory_space=pltpu.VMEM),
        scratch_shapes=[pltpu.VMEM((members + ncells + 8, members), jnp.float32)],
        compiler_params=pltpu.CompilerParams(vmem_limit_bytes=32 << 20),
    )(packed, cells, mean_col)


def packed_rows(members, ways):
    need = 8
    for j in range(members // BLK):
        need += members - j * BLK
    step = 8 * ways
    return (need + step - 1) // step * step


def bits_of(n):
    return [1 << t for t in range(n.bit_length() - 1)]


def observe_kernel(
    obs_n, state_n, ids_ref, counts_ref, cells_ref, mean_ref, ops_ref, read_ref, std_ref, out_ref,
    slab, slab_mean, part, sent, got, inno, inno_got, acc, acc_got, full,
    right_send, right_recv, left_send, left_recv, part_send, part_recv, acc_send, acc_recv,
):
    me_o, me_s = lax.axis_index("obs"), lax.axis_index("state")
    nb, slots = ops_ref.shape[0], ops_ref.shape[1]
    members = cells_ref.shape[1]
    state_bits, obs_bits = bits_of(state_n), bits_of(obs_n)

    def partner(axis, bit):
        me = me_s if axis == "state" else me_o
        return me + bit - 2 * bit * ((me // bit) % 2)

    slab[me_o] = cells_ref[...]
    slab_mean[me_o] = jnp.broadcast_to(mean_ref[...], (16, BLK)).astype(jnp.bfloat16)

    barrier = pltpu.get_barrier_semaphore()
    greeted = [{"obs": lax.rem(me_o + 1, obs_n)}, {"obs": lax.rem(me_o + obs_n - 1, obs_n)}]
    greeted += [{"obs": partner("obs", b)} for b in obs_bits]
    greeted += [{"state": partner("state", b)} for b in state_bits]
    for where in greeted:
        pl.semaphore_signal(barrier, inc=1, device_id=where, device_id_type=pl.DeviceIdType.MESH)
    pl.semaphore_wait(barrier, len(greeted))

    def remote(src, dst, send, recv, where):
        return pltpu.make_async_remote_copy(
            src_ref=src, dst_ref=dst, send_sem=send, recv_sem=recv,
            device_id=where, device_id_type=pl.DeviceIdType.MESH,
        )

    def hop(block, sends, recvs, t, to):
        return [
            remote(slab.at[block], slab.at[block], sends.at[0, t], recvs.at[0, t], {"obs": to}),
            remote(slab_mean.at[block], slab_mean.at[block], sends.at[1, t], recvs.at[1, t], {"obs": to}),
        ]

    def clip(x):
        return jnp.clip(x, 0, obs_n - 1)

    for t in range(obs_n - 1):
        @pl.when((me_o < obs_n - 1) & (me_o - t >= 0))
        def _():
            for c in hop(clip(me_o - t), right_send, right_recv, t, clip(me_o + 1)):
                c.start()

        @pl.when((me_o > 0) & (me_o + t <= obs_n - 1))
        def _():
            for c in hop(clip(me_o + t), left_send, left_recv, t, clip(me_o - 1)):
                c.start()

        @pl.when(me_o - 1 - t >= 0)
        def _():
            for c in hop(clip(me_o - 1 - t), right_send, right_recv, t, clip(me_o - 1)):
                c.wait_recv()

        @pl.when(me_o + 1 + t <= obs_n - 1)
        def _():
            for c in hop(clip(me_o + 1 + t), left_send, left_recv, t, clip(me_o + 1)):
                c.wait_recv()

    lane = lax.broadcasted_iota(jnp.int32, (1, BLK), 1)

    def observe(b):
        rows = jnp.zeros((BLK, members), jnp.float32)
        mean = jnp.zeros((16, BLK), jnp.float32)
        for j in range(slots):
            column = ids_ref[b, j]
            op = ops_ref[b, j]
            rows += jnp.dot(op, slab[column], preferred_element_type=jnp.float32)
            mean += lax.dot_general(slab_mean[column], op, NT, preferred_element_type=jnp.float32)
        weight = jnp.where(lane < counts_ref[b], 1.0 / std_ref[pl.ds(b, 1), :], 0.0)
        inno[pl.ds(b, 1), :] = weight * (read_ref[pl.ds(b, 1), :] * (1.0 / state_n) - mean[0:1])
        return rows * jnp.broadcast_to(weight, (BLK, BLK)).T[:, 0:1]

    half = nb // 2
    low = 0
    for t, bit in enumerate(state_bits):
        high_bit = (me_s // bit) % 2
        keep = high_bit * half
        give = half - keep
        if t == 0:
            @pl.loop(0, half)
            def _(i):
                sent[i] = observe(give + i).astype(jnp.bfloat16)
        else:
            sent[0:half] = part[pl.ds(low + give, half)].astype(jnp.bfloat16)
        off = 0 if t == 0 else nb - 2 * half
        where = {"state": partner("state", bit)}
        copy = remote(
            sent.at[pl.ds(0, half)], got.at[pl.ds(off, half)], part_send.at[0, t], part_recv.at[0, t], where
        )
        copy.start()
        if t == 0:
            @pl.loop(0, half)
            def _(i):
                part[keep + i] = observe(keep + i)
        small = remote(inno, inno_got.at[t], part_send.at[1, t], part_recv.at[1, t], where)
        small.start()
        copy.wait()
        small.wait()
        low = low + keep
        part[pl.ds(low, half)] += got[off : off + half].astype(jnp.float32)
        inno[...] += inno_got[t]
        half //= 2
    own = nb // state_n

    scaled = part[pl.ds(low, own)].reshape(own * BLK, members)
    row = 0
    for j in range(members // BLK):
        size = members - j * BLK
        acc[row : row + size, :] = lax.dot_general(
            scaled[:, j * BLK :], scaled[:, j * BLK : (j + 1) * BLK], (((0,), (0,)), ((), ())),
            precision=HI, preferred_element_type=jnp.float32,
        )
        row += size
    rhs = jnp.zeros((8, members), jnp.float32)
    for i in range(own):
        rhs += jnp.dot(
            jnp.broadcast_to(inno[pl.ds(low + i, 1), :], (8, BLK)), scaled[i * BLK : (i + 1) * BLK],
            precision=HI, preferred_element_type=jnp.float32,
        )
    acc[row:, :] = jnp.zeros((acc.shape[0] - row, BLK), jnp.float32)
    for j in range(members // BLK):
        acc[row + j : row + j + 1, :] = rhs[0:1, j * BLK : (j + 1) * BLK]

    steps = [("state", b) for b in state_bits] + [("obs", b) for b in obs_bits]
    size = acc.shape[0]
    base = 0
    spot = 0
    trail = []
    for n, (axis, bit) in enumerate(steps):
        size //= 2
        keep = ((me_s if axis == "state" else me_o) // bit) % 2 * size
        where = {axis: partner(axis, bit)}
        give = pl.multiple_of(base + size - keep, 8)
        copy = remote(
            acc.at[pl.ds(give, size)], acc_got.at[pl.ds(spot, size)], acc_send.at[n], acc_recv.at[n], where
        )
        copy.start()
        copy.wait()
        base = pl.multiple_of(base + keep, 8)
        acc[pl.ds(base, size), :] += acc_got[spot : spot + size, :]
        spot += size
        trail.append((n, where, base, size))
    full[pl.ds(base, size), :] = acc[pl.ds(base, size), :]
    for n, where, base, size in reversed(trail):
        m = len(steps) + n
        copy = remote(
            full.at[pl.ds(base, size)], full.at[pl.ds(base, size)], acc_send.at[m], acc_recv.at[m], where
        )
        copy.start()
        copy.wait()

    for t in range(obs_n - 1):
        @pl.when((me_o < obs_n - 1) & (me_o - t >= 0))
        def _():
            for c in hop(clip(me_o - t), right_send, right_recv, t, clip(me_o + 1)):
                c.wait_send()

        @pl.when((me_o > 0) & (me_o + t <= obs_n - 1))
        def _():
            for c in hop(clip(me_o + t), left_send, left_recv, t, clip(me_o - 1)):
                c.wait_send()
    out_ref[...] = full[...]


def observe(obs_n, state_n, ids, counts, cells, mean_row, ops, readings, stds):
    nb = ops.shape[0]
    members = cells.shape[1]
    rows = packed_rows(members, obs_n * state_n)
    nsteps = 2 * (len(bits_of(obs_n)) + len(bits_of(state_n)))
    hops = pltpu.SemaphoreType.DMA((2, obs_n - 1))
    pieces = pltpu.SemaphoreType.DMA((2, len(bits_of(state_n))))
    return pl.pallas_call(
        functools.partial(observe_kernel, obs_n, state_n),
        out_shape=jax.ShapeDtypeStruct((rows, BLK), jnp.float32),
        in_specs=[pl.BlockSpec(memory_space=pltpu.SMEM)] * 2
        + [pl.BlockSpec(memory_space=pltpu.VMEM)] * 5,
        out_specs=pl.BlockSpec(memory_space=pltpu.VMEM),
        scratch_shapes=[
            pltpu.VMEM((obs_n, BLK, members), jnp.bfloat16),
            pltpu.VMEM((obs_n, 16, BLK), jnp.bfloat16),
            pltpu.VMEM((nb, BLK, members), jnp.float32),
            pltpu.VMEM((nb // 2, BLK, members), jnp.bfloat16),
            pltpu.VMEM((nb, BLK, members), jnp.bfloat16),
            pltpu.VMEM((nb, BLK), jnp.float32),
            pltpu.VMEM((len(bits_of(state_n)), nb, BLK), jnp.float32),
            pltpu.VMEM((rows, BLK), jnp.float32),
            pltpu.VMEM((rows, BLK), jnp.float32),
            pltpu.VMEM((rows, BLK), jnp.float32),
            hops, hops, hops, hops, pieces, pieces,
            pltpu.SemaphoreType.DMA((nsteps,)),
            pltpu.SemaphoreType.DMA((nsteps,)),
        ],
        compiler_params=pltpu.CompilerParams(
            collective_id=0, has_side_effects=True, vmem_limit_bytes=48 << 20
        ),
    )(ids, counts, cells, mean_row, ops, readings, stds)


def local(
    obs_n,
    state_n,
    anomalies,
    prior_ensemble_mean,
    operator_blocks,
    block_column_ids,
    observation_counts,
    observed_readings,
    observation_error_std,
):
    cells = anomalies[0]
    packed = observe(
        obs_n, state_n, block_column_ids[:, 0], observation_counts, cells, prior_ensemble_mean,
        operator_blocks[:, 0], observed_readings, observation_error_std,
    )
    return finish(packed, cells, prior_ensemble_mean.reshape(-1, 1))[None]


def solution(mesh):
    placed = (
        P("state", "obs", None),
        P("state", "obs"),
        P(("net", "obs"), "state", None, None, None),
        P(("net", "obs"), "state", None),
        P(("net", "obs")),
        P(("net", "obs"), None),
        P(("net", "obs"), None),
    )
    return jax.shard_map(
        functools.partial(local, mesh.shape["obs"], mesh.shape["state"]),
        mesh=mesh,
        in_specs=placed,
        out_specs=P(("net", "state"), "obs", None),
        check_vma=False,
    )
```

time: 246 us -> 119 us (0.48)
  waiting for transfers between devices: 82.8 us -> 0 us
  Pallas kernels: 50.9 us -> 112 us
  blocking collectives: 46.7 us -> 0 us
  matrix products: 33.5 us -> 0 us
  between operations: 13.5 us -> 0.02 us
  other arithmetic: 7.69 us -> 0 us
  local copies, waits for them, and re-layouts: 9.87 us -> 6.62 us
    psum x2 -> x0, waiting for transfers between devices: 82.7 us -> none  [the longest x1 43.9 us: local(): obs_anom, obs_mean = lax.psum((part_anom, part_mean), 'state')]
    pallas_call x0 -> x1, Pallas kernels: none -> 61.4 us  [observe(): pl.pallas_call(functools.partial(observe_kernel, obs_n, state_n), out_sha...]
    dot_general x18 -> x0, matrix products: 33.5 us -> none  [the longest x8 15.8 us: one_block(): jnp.einsum('jrc,jck->rk', values, picked, preferred_element_type=jnp.floa...]
    all_gather x2 -> x0, blocking collectives: 29.2 us -> none  [the longest x1 17.6 us: local(): lax.all_gather(local_cells, 'obs', axis=0, tiled=True)]
    psum x2 -> x0, blocking collectives: 17.5 us -> none  [the longest x1 11.9 us: local(): gram, rhs = lax.psum((gram_part, rhs_part), 'obs')]
    gather x16 -> x0, local copies, waits for them, and re-layouts: 9.49 us -> none  [the longest x8 4.98 us: one_block(): picked = cells[columns]]
    unnamed x12 -> x14, local copies, waits for them, and re-layouts: 0.02 us -> 5.86 us
    select_n x8 -> x0, other arithmetic: 5.55 us -> none  [one_block(): picked = cells[columns]]
  transfers between devices with their start and end apart: 2 -> 0, of which waited for: 2 -> 0; matrix products, arithmetic and copies ran while one was open for 1% -> 0% of each run, Pallas kernels for 0% -> 0%
where the time goes in v2:
time: 119 us
  Pallas kernels  112 us (94%)
  local copies, waits for them, and re-layouts  6.62 us (6%)
    pallas_call x1, Pallas kernels, observe(): pl.pallas_call(functools.partial(observe_kernel, obs_n, state_n), out_sha...  61.4 us
    pallas_call x1, Pallas kernels, finish(): pl.pallas_call(finish_kernel, out_shape=jax.ShapeDtypeStruct((ncells, mem...  51 us
    unnamed x14, local copies, waits for them, and re-layouts  5.86 us

profile of v2, /device:TPU:0, one launch (start us, length us, event | category | flops | bytes accessed | tf_op | source)
XLA Modules:
  0.0 119.0 jit_solution(18355712257788684845)
XLA Ops:
  0.0 0.8 copy.8.mean_ref
  0.8 0.0 copy-start
  0.8 1.6 %copy-done = bf16[8,1,8,128,128]{4,3,2,1,0:T(8,128)(2,1)S(1)} copy-done((bf16[8,1,8,128,128]{4,3,2,1,0:T(8,128)(2,1)S(1)}, bf16[8,1,8,128,128]{4,3,2,1,0:T(8,128)(2,1)}, u32[]{:S(2)}) %copy-start) | copy-done | bytes 2097176
  2.4 0.0 copy-start.1
  2.4 0.9 copy-done.1
  3.3 0.0 copy-start.2
  3.3 0.7 copy-done.2
  3.9 0.0 copy-start.3
  3.9 0.7 copy-done.3
  4.6 0.0 copy-start.4
  4.6 0.7 copy-done.4
  5.3 0.0 copy-start.5
  5.3 0.7 copy-done.5
  6.0 0.0 copy-start.6
  6.0 0.7 copy-done.6
  6.6 61.4 %shard_map.73.packed_ref = f32[1408,128]{1,0:T(8,128)S(1)} custom-call(s32[8,8]{1,0:T(8,128)S(1)} %bitcast.8, s32[8]{0:T(128)S(1)} %copy-done.6, bf16[128,512]{1,0:T(8,128)(2,1)S(1)} %bitcast.6, f32[1,128]{1,0:T(1,128)S(1)} %copy-done.5, bf16[8,8,128,128]{3,2,1,0:T(8,128)(2,1)S(1)} %bitcast.5, f32[8,128]{1,0:T(8,128)S(1)} %copy-done.3, f32[8,128]{1,0:T(8,128)S(1)} %copy-done.4), custom_call_target="tpu_custom_call" | custom-call | tf_op jit(solution)/shard_map/pallas_call | solution.py:283
  68.1 51.0 %shard_map.74 = bf16[128,512]{1,0:T(8,128)(2,1)} custom-call(f32[1408,128]{1,0:T(8,128)S(1)} %shard_map.73.packed_ref, bf16[128,512]{1,0:T(8,128)(2,1)S(1)} %bitcast.7, f32[128,1]{1,0:T(8,128)S(1)} %copy.8.mean_ref), custom_call_target="tpu_custom_call" | custom-call | tf_op jit(solution)/shard_map/pallas_call | solution.py:87
Async XLA Ops:
  0.8 1.6 %copy-start = (bf16[8,1,8,128,128]{4,3,2,1,0:T(8,128)(2,1)S(1)}, bf16[8,1,8,128,128]{4,3,2,1,0:T(8,128)(2,1)}, u32[]{:S(2)}) copy-start(bf16[8,1,8,128,128]{4,3,2,1,0:T(8,128)(2,1)} %param.9) | copy-start | bytes 6291460
  2.4 0.9 copy-start.1
  3.3 0.7 copy-start.2
  3.9 0.7 copy-start.3
  4.6 0.7 copy-start.4
  5.3 0.7 copy-start.5
  6.0 0.7 copy-start.6

commit v3 on v2

v3 whole, which is shorter than its diff:
```python
import functools
import jax
import jax.numpy as jnp
from jax import lax
from jax.experimental import pallas as pl
from jax.experimental.pallas import tpu as pltpu
from jax.sharding import PartitionSpec as P

BLK = 128
HI = lax.Precision.HIGHEST
NT = (((1,), (1,)), ((), ()))


def inverse_factor(block, width=32):
    row = lax.broadcasted_iota(jnp.int32, (BLK, BLK), 0)
    col = lax.broadcasted_iota(jnp.int32, (BLK, BLK), 1)
    eye = (row == col).astype(jnp.float32)
    groups = BLK // 8
    left = [block[8 * g : 8 * g + 8] for g in range(groups)]
    right = [eye[8 * g : 8 * g + 8] for g in range(groups)]
    sub = lax.broadcasted_iota(jnp.int32, (8, 1), 0)
    lane = lax.broadcasted_iota(jnp.int32, (1, BLK), 1)
    local = width // 8
    for start in range(0, BLK, width):
        g0 = start // 8
        spread = [
            [jnp.broadcast_to(left[g0 + h][:, start + j : start + j + 1], (8, BLK)) for h in range(local)]
            for j in range(width)
        ]
        scaled = []
        roots = []
        for j in range(width):
            gj, ij = divmod(j, 8)
            pivot = spread[j][gj][ij : ij + 1]
            inv = 1.0 / pivot
            lrow = left[g0 + gj][ij : ij + 1] * inv
            rrow = right[g0 + gj][ij : ij + 1] * inv
            scaled.append(lrow)
            roots.append(lax.rsqrt(pivot))
            shared = [None if t <= j else spread[t][gj][ij : ij + 1] * inv for t in range(width)]
            for h in range(gj, local):
                m = spread[j][h]
                if h == gj:
                    if ij == 7:
                        continue
                    m = jnp.where(sub > ij, m, 0.0)
                for t in range(j + 1, width):
                    spread[t][h] = spread[t][h] - m * shared[t]
                left[g0 + h] = left[g0 + h] - m * lrow
                right[g0 + h] = right[g0 + h] - m * rrow
        upper_l = jnp.concatenate(left[g0 : g0 + local], axis=0)
        upper_r = jnp.concatenate(right[g0 : g0 + local], axis=0)
        end = start + width
        if end < BLK:
            low = jnp.where(lane >= end, jnp.concatenate(scaled, axis=0), 0.0)
            change = lax.dot_general(
                low, jnp.concatenate([upper_l, upper_r], axis=1), (((0,), (0,)), ((), ())),
                precision=HI, preferred_element_type=jnp.float32,
            )
            for h in range(end // 8, groups):
                left[h] = left[h] - change[8 * h : 8 * h + 8, :BLK]
                right[h] = right[h] - change[8 * h : 8 * h + 8, BLK:]
        scale = jnp.concatenate(roots, axis=0)
        for h in range(local):
            right[g0 + h] = right[g0 + h] * scale[8 * h : 8 * h + 8]
    return jnp.concatenate(right, axis=0)


def finish_kernel(packed_ref, anom_ref, mean_ref, out_ref, work):
    cells, members = anom_ref.shape
    total = members + cells + 8
    row = lax.broadcasted_iota(jnp.int32, (BLK, BLK), 0)
    col = lax.broadcasted_iota(jnp.int32, (BLK, BLK), 1)
    ridge = jnp.where(row == col, members - 1.0, 0.0)
    start = 0
    last = packed_ref.shape[0] - 8
    for j in range(members // BLK):
        size = members - j * BLK
        cols = slice(j * BLK, (j + 1) * BLK)
        if j:
            work[0 : j * BLK, cols] = jnp.zeros((j * BLK, BLK), jnp.float32)
        work[cols, cols] = packed_ref[start : start + BLK, :] + ridge
        if size > BLK:
            work[(j + 1) * BLK : members, cols] = packed_ref[start + BLK : start + size, :]
        start += size
    for j in range(members // BLK):
        cols = slice(j * BLK, (j + 1) * BLK)
        work[members + cells : total, cols] = jnp.broadcast_to(
            packed_ref[last + j : last + j + 1, :], (8, BLK)
        )
    work[members : members + cells, :] = anom_ref[...].astype(jnp.float32)

    @pl.loop(0, members // BLK)
    def _(p):
        off = pl.multiple_of(p * BLK, BLK)
        inv = inverse_factor(work[pl.ds(off, BLK), pl.ds(off, BLK)])
        x = lax.dot_general(
            work[:, pl.ds(off, BLK)], inv, NT, precision=HI, preferred_element_type=jnp.float32
        )
        rows = lax.broadcasted_iota(jnp.int32, (total, 1), 0)
        x = jnp.where(rows >= off + BLK, x, 0.0)
        work[...] -= lax.dot_general(
            x, x[:members], NT, precision=HI, preferred_element_type=jnp.float32
        )
        work[members:total, pl.ds(off, BLK)] = x[members:]

    solved = work[members : members + cells, :]
    shift = jnp.sum(solved * work[members + cells : members + cells + 1, :], axis=1, keepdims=True)
    root = (members - 1.0) ** 0.5
    mean = jnp.broadcast_to(mean_ref[...], (BLK, cells)).T[:, 0:1]
    out_ref[...] = (mean + (root * solved + shift)).astype(jnp.bfloat16)


def finish(packed, cells, mean_row):
    ncells, members = cells.shape
    return pl.pallas_call(
        finish_kernel,
        out_shape=jax.ShapeDtypeStruct((ncells, members), jnp.bfloat16),
        in_specs=[pl.BlockSpec(memory_space=pltpu.VMEM)] * 3,
        out_specs=pl.BlockSpec(memory_space=pltpu.VMEM),
        scratch_shapes=[pltpu.VMEM((members + ncells + 8, members), jnp.float32)],
        compiler_params=pltpu.CompilerParams(vmem_limit_bytes=32 << 20),
    )(packed, cells, mean_row)


def packed_rows(members, ways):
    need = sum(members - j * BLK for j in range(members // BLK))
    step = 16 * ways
    return (need + step - 1) // step * step


def bits_of(n):
    return [1 << t for t in range(n.bit_length() - 1)]


def observe_kernel(
    obs_n, state_n, ids_ref, counts_ref, cells_hbm, mean_hbm, ops_hbm, read_hbm, std_hbm, out_ref,
    mean_row, ops_ref, read_ref, std_ref, load_sem,
    slab, slab_mean, part, sent, got, inno, inno_got, acc, acc_got, full, rhs_sum, rhs_got,
    right_send, right_recv, left_send, left_recv, part_send, part_recv, inno_send, inno_recv,
    acc_send, acc_recv, rhs_send, rhs_recv,
):
    me_o, me_s = lax.axis_index("obs"), lax.axis_index("state")
    nb, slots = ops_ref.shape[0], ops_ref.shape[1]
    members = slab.shape[2]
    state_bits, obs_bits = bits_of(state_n), bits_of(obs_n)

    loads = [
        pltpu.make_async_copy(src, dst, load_sem.at[n])
        for n, (src, dst) in enumerate([
            (cells_hbm, slab.at[me_o]), (mean_hbm, mean_row), (read_hbm, read_ref),
            (std_hbm, std_ref), (ops_hbm, ops_ref),
        ])
    ]
    for load in loads:
        load.start()

    def partner(axis, bit):
        me = me_s if axis == "state" else me_o
        return me + bit - 2 * bit * ((me // bit) % 2)

    barrier = pltpu.get_barrier_semaphore()
    greeted = [{"obs": lax.rem(me_o + 1, obs_n)}, {"obs": lax.rem(me_o + obs_n - 1, obs_n)}]
    greeted += [{"obs": partner("obs", b)} for b in obs_bits]
    greeted += [{"state": partner("state", b)} for b in state_bits]
    for where in greeted:
        pl.semaphore_signal(barrier, inc=1, device_id=where, device_id_type=pl.DeviceIdType.MESH)
    loads[0].wait()
    loads[1].wait()
    slab_mean[me_o] = jnp.broadcast_to(mean_row[...], (16, BLK)).astype(jnp.bfloat16)
    pl.semaphore_wait(barrier, len(greeted))

    def remote(src, dst, send, recv, where):
        return pltpu.make_async_remote_copy(
            src_ref=src, dst_ref=dst, send_sem=send, recv_sem=recv,
            device_id=where, device_id_type=pl.DeviceIdType.MESH,
        )

    def hop(block, sends, recvs, t, to):
        return [
            remote(slab.at[block], slab.at[block], sends.at[0, t], recvs.at[0, t], {"obs": to}),
            remote(slab_mean.at[block], slab_mean.at[block], sends.at[1, t], recvs.at[1, t], {"obs": to}),
        ]

    def clip(x):
        return jnp.clip(x, 0, obs_n - 1)

    for t in range(obs_n - 1):
        @pl.when((me_o < obs_n - 1) & (me_o - t >= 0))
        def _():
            for c in hop(clip(me_o - t), right_send, right_recv, t, clip(me_o + 1)):
                c.start()

        @pl.when((me_o > 0) & (me_o + t <= obs_n - 1))
        def _():
            for c in hop(clip(me_o + t), left_send, left_recv, t, clip(me_o - 1)):
                c.start()

        @pl.when(me_o - 1 - t >= 0)
        def _():
            for c in hop(clip(me_o - 1 - t), right_send, right_recv, t, clip(me_o - 1)):
                c.wait_recv()

        @pl.when(me_o + 1 + t <= obs_n - 1)
        def _():
            for c in hop(clip(me_o + 1 + t), left_send, left_recv, t, clip(me_o + 1)):
                c.wait_recv()

    for load in loads[2:]:
        load.wait()
    lane = lax.broadcasted_iota(jnp.int32, (1, BLK), 1)

    def weight_of(b):
        return jnp.where(lane < counts_ref[b], 1.0 / std_ref[pl.ds(b, 1), :], 0.0)

    @pl.loop(0, nb)
    def _(b):
        mean = jnp.zeros((16, BLK), jnp.float32)
        for j in range(slots):
            mean += lax.dot_general(
                slab_mean[ids_ref[b, j]], ops_ref[b, j], NT, preferred_element_type=jnp.float32
            )
        share = read_ref[pl.ds(b, 1), :] * (1.0 / state_n)
        inno[pl.ds(b, 1), :] = weight_of(b) * (share - mean[0:1])

    def inno_copy(t):
        where = {"state": partner("state", state_bits[t])}
        return remote(inno, inno_got.at[t], inno_send.at[t], inno_recv.at[t], where)

    inno_copy(0).start()

    def observe(b):
        rows = jnp.zeros((BLK, members), jnp.float32)
        for j in range(slots):
            rows += jnp.dot(ops_ref[b, j], slab[ids_ref[b, j]], preferred_element_type=jnp.float32)
        return rows * jnp.broadcast_to(weight_of(b), (BLK, BLK)).T[:, 0:1]

    def part_copy(t, i):
        n = nb - (nb >> t) + i
        where = {"state": partner("state", state_bits[t])}
        return remote(sent.at[n], got.at[n], part_send.at[n], part_recv.at[n], where)

    lows = [0]
    for t, bit in enumerate(state_bits):
        half = nb >> (t + 1)
        keep = (me_s // bit) % 2 * half
        give = lows[-1] + half - keep
        lows.append(lows[-1] + keep)

        def total(b, upto):
            value = observe(b)
            for u in range(upto):
                part_copy(u, b - lows[u + 1]).wait_recv()
                value += got[nb - (nb >> u) + b - lows[u + 1]].astype(jnp.float32)
            return value

        @pl.loop(0, half)
        def _(i):
            sent[nb - (nb >> t) + i] = total(give + i, t).astype(jnp.bfloat16)
            part_copy(t, i).start()

        inno_copy(t).wait()
        inno[...] += inno_got[t]
        if t + 1 < len(state_bits):
            inno_copy(t + 1).start()
    own = nb // state_n
    low = lows[-1]
    last = len(state_bits) - 1

    @pl.loop(0, own)
    def _(i):
        value = observe(low + i)
        for u in range(last):
            part_copy(u, low + i - lows[u + 1]).wait_recv()
            value += got[nb - (nb >> u) + low + i - lows[u + 1]].astype(jnp.float32)
        part[i] = value

    @pl.loop(0, own)
    def _(i):
        part_copy(last, i).wait_recv()
        part[i] += got[nb - (nb >> last) + i].astype(jnp.float32)

    scaled = part[...].reshape(own * BLK, members)
    row = 0
    for j in range(members // BLK):
        size = members - j * BLK
        acc[row : row + size, :] = lax.dot_general(
            scaled[:, j * BLK :], scaled[:, j * BLK : (j + 1) * BLK], (((0,), (0,)), ((), ())),
            precision=HI, preferred_element_type=jnp.float32,
        )
        row += size
    if row < acc.shape[0]:
        acc[row:, :] = jnp.zeros((acc.shape[0] - row, BLK), jnp.float32)
    rhs = jnp.zeros((8, members), jnp.float32)
    for i in range(own):
        rhs += jnp.dot(
            jnp.broadcast_to(inno[pl.ds(low + i, 1), :], (8, BLK)), scaled[i * BLK : (i + 1) * BLK],
            precision=HI, preferred_element_type=jnp.float32,
        )
    rhs_sum[...] = jnp.zeros((8, BLK), jnp.float32)
    for j in range(members // BLK):
        rhs_sum[j : j + 1, :] = rhs[0:1, j * BLK : (j + 1) * BLK]

    by_state = [("state", b) for b in state_bits]
    by_obs = [("obs", b) for b in obs_bits]
    orders = [by_state + by_obs, by_state[:1] + by_obs + by_state[1:]]
    steps = len(orders[0])
    size = acc.shape[0] // 2
    bases = [0, size]
    spots = [0, size]
    trail = []
    for n in range(steps):
        size //= 2
        copies = []
        for k in range(2):
            axis, bit = orders[k][n]
            keep = ((me_s if axis == "state" else me_o) // bit) % 2 * size
            where = {axis: partner(axis, bit)}
            give = pl.multiple_of(bases[k] + size - keep, 8)
            copies.append(remote(
                acc.at[pl.ds(give, size)], acc_got.at[pl.ds(spots[k], size)],
                acc_send.at[k, n], acc_recv.at[k, n], where,
            ))
            bases[k] = pl.multiple_of(bases[k] + keep, 8)
            trail.append((k, n, where, bases[k], size))
            if k == 0:
                copies.append(remote(rhs_sum, rhs_got.at[n], rhs_send.at[n], rhs_recv.at[n], where))
        for copy in copies:
            copy.start()
        for copy in copies:
            copy.wait()
        for k in range(2):
            acc[pl.ds(bases[k], size), :] += acc_got[spots[k] : spots[k] + size, :]
            spots[k] += size
        rhs_sum[...] += rhs_got[n]
    for k in range(2):
        full[pl.ds(bases[k], size), :] = acc[pl.ds(bases[k], size), :]
    for n in reversed(range(steps)):
        copies = [
            remote(
                full.at[pl.ds(base, size)], full.at[pl.ds(base, size)],
                acc_send.at[k, steps + n], acc_recv.at[k, steps + n], where,
            )
            for k, m, where, base, size in trail if m == n
        ]
        for copy in copies:
            copy.start()
        for copy in copies:
            copy.wait()

    for t in range(obs_n - 1):
        @pl.when((me_o < obs_n - 1) & (me_o - t >= 0))
        def _():
            for c in hop(clip(me_o - t), right_send, right_recv, t, clip(me_o + 1)):
                c.wait_send()

        @pl.when((me_o > 0) & (me_o + t <= obs_n - 1))
        def _():
            for c in hop(clip(me_o + t), left_send, left_recv, t, clip(me_o - 1)):
                c.wait_send()
    for t in range(len(state_bits)):
        for i in range(nb >> (t + 1)):
            part_copy(t, i).wait_send()
    out_ref[0 : full.shape[0], :] = full[...]
    out_ref[full.shape[0] :, :] = rhs_sum[...]


def observe(obs_n, state_n, ids, counts, cells, mean_row, ops, readings, stds):
    nb = ops.shape[0]
    members = cells.shape[1]
    rows = packed_rows(members, obs_n * state_n)
    rounds = len(bits_of(state_n))
    steps = len(bits_of(obs_n)) + rounds
    hops = pltpu.SemaphoreType.DMA((2, obs_n - 1))
    dma = lambda *shape: pltpu.SemaphoreType.DMA(shape)
    return pl.pallas_call(
        functools.partial(observe_kernel, obs_n, state_n),
        out_shape=jax.ShapeDtypeStruct((rows + 8, BLK), jnp.float32),
        in_specs=[pl.BlockSpec(memory_space=pltpu.SMEM)] * 2
        + [pl.BlockSpec(memory_space=pl.ANY)] * 5,
        out_specs=pl.BlockSpec(memory_space=pltpu.VMEM),
        scratch_shapes=[
            pltpu.VMEM(mean_row.shape, jnp.float32),
            pltpu.VMEM(ops.shape, jnp.bfloat16),
            pltpu.VMEM((nb, BLK), jnp.float32),
            pltpu.VMEM((nb, BLK), jnp.float32),
            dma(5),
            pltpu.VMEM((obs_n, BLK, members), jnp.bfloat16),
            pltpu.VMEM((obs_n, 16, BLK), jnp.bfloat16),
            pltpu.VMEM((nb // state_n, BLK, members), jnp.float32),
            pltpu.VMEM((nb, BLK, members), jnp.bfloat16),
            pltpu.VMEM((nb, BLK, members), jnp.bfloat16),
            pltpu.VMEM((nb, BLK), jnp.float32),
            pltpu.VMEM((rounds, nb, BLK), jnp.float32),
            pltpu.VMEM((rows, BLK), jnp.float32),
            pltpu.VMEM((rows, BLK), jnp.float32),
            pltpu.VMEM((rows, BLK), jnp.float32),
            pltpu.VMEM((8, BLK), jnp.float32),
            pltpu.VMEM((steps, 8, BLK), jnp.float32),
            hops, hops, hops, hops,
            dma(nb), dma(nb), dma(rounds), dma(rounds),
            dma(2, 2 * steps), dma(2, 2 * steps), dma(steps), dma(steps),
        ],
        compiler_params=pltpu.CompilerParams(
            collective_id=0, has_side_effects=True, vmem_limit_bytes=60 << 20
        ),
    )(ids, counts, cells, mean_row, ops, readings, stds)


def local(
    obs_n,
    state_n,
    anomalies,
    prior_ensemble_mean,
    operator_blocks,
    block_column_ids,
    observation_counts,
    observed_readings,
    observation_error_std,
):
    cells = anomalies[0]
    packed = observe(
        obs_n, state_n, block_column_ids[:, 0], observation_counts, cells, prior_ensemble_mean,
        operator_blocks[:, 0], observed_readings, observation_error_std,
    )
    return finish(packed, cells, prior_ensemble_mean)[None]


def solution(mesh):
    placed = (
        P("state", "obs", None),
        P("state", "obs"),
        P(("net", "obs"), "state", None, None, None),
        P(("net", "obs"), "state", None),
        P(("net", "obs")),
        P(("net", "obs"), None),
        P(("net", "obs"), None),
    )
    return jax.shard_map(
        functools.partial(local, mesh.shape["obs"], mesh.shape["state"]),
        mesh=mesh,
        in_specs=placed,
        out_specs=P(("net", "state"), "obs", None),
        check_vma=False,
    )
```

time: 119 us -> 84.3 us (0.71)
  Pallas kernels: 112 us -> 83 us
  local copies, waits for them, and re-layouts: 6.62 us -> 1.09 us
    pallas_call x1, Pallas kernels: 51 us -> 25.1 us  [finish(): pl.pallas_call(finish_kernel, out_shape=jax.ShapeDtypeStruct((ncells, mem...]
    unnamed x14 -> x6, local copies, waits for them, and re-layouts: 5.86 us -> 1.09 us
    pallas_call x1, Pallas kernels: 61.4 us -> 58 us  [observe(): pl.pallas_call(functools.partial(observe_kernel, obs_n, state_n), out_sha...]
where the time goes in v3:
time: 84.3 us; the launch traced here: 84.2 us
  Pallas kernels  83 us (98%)
  local copies, waits for them, and re-layouts  1.09 us (1%)
    pallas_call x1, Pallas kernels, observe(): pl.pallas_call(functools.partial(observe_kernel, obs_n, state_n), out_sha...  58 us
    pallas_call x1, Pallas kernels, finish(): pl.pallas_call(finish_kernel, out_shape=jax.ShapeDtypeStruct((ncells, mem...  25.1 us

profile of v3, /device:TPU:0, one launch (start us, length us, event | category | flops | bytes accessed | tf_op | source)
XLA Modules:
  0.0 84.2 jit_solution(13746683988380709916)
XLA Ops:
  0.0 0.0 copy-start.2
  0.0 0.0 copy-start.1
  0.0 58.0 %shard_map.73.packed_ref = f32[1288,128]{1,0:T(8,128)} custom-call(s32[8,8]{1,0:T(8,128)} %bitcast.7, s32[8]{0:T(128)} %counts_ref.1, bf16[128,512]{1,0:T(8,128)(2,1)} %bitcast.4, f32[1,128]{1,0:T(1,128)} %mean_ref.1, bf16[8,8,128,128]{3,2,1,0:T(8,128)(2,1)} %bitcast.6, f32[8,128]{1,0:T(8,128)} %read_hbm.1, f32[8,128]{1,0:T(8,128)} %std_hbm.1), custom_call_target="tpu_custom_call" | custom-call | tf_op jit(solution)/shard_map/pallas_call | solution.py:376
  58.0 0.0 copy-done.2
  58.0 0.0 copy-done.1
  58.0 0.0 copy-start
  58.0 1.1 %copy-done = f32[1288,128]{1,0:T(8,128)S(1)} copy-done((f32[1288,128]{1,0:T(8,128)S(1)}, f32[1288,128]{1,0:T(8,128)}, u32[]{:S(2)}) %copy-start) | copy-done | bytes 659480
  59.1 25.1 %shard_map.74 = bf16[128,512]{1,0:T(8,128)(2,1)} custom-call(f32[1288,128]{1,0:T(8,128)S(1)} %copy-done, bf16[128,512]{1,0:T(8,128)(2,1)S(1)} %bitcast.5, f32[1,128]{1,0:T(1,128)S(1)} %copy-done.2), custom_call_target="tpu_custom_call" | custom-call | tf_op jit(solution)/shard_map/pallas_call | solution.py:116
Async XLA Ops:
  0.0 58.0 %copy-start.2 = (f32[1,128]{1,0:T(1,128)S(1)}, f32[1,128]{1,0:T(1,128)}, u32[]{:S(2)}) copy-start(f32[1,128]{1,0:T(1,128)} %mean_ref.1) | copy-start | bytes 1540
  0.0 58.0 %copy-start.1 = (bf16[1,128,512]{2,1,0:T(8,128)(2,1)S(1)}, bf16[1,128,512]{2,1,0:T(8,128)(2,1)}, u32[]{:S(2)}) copy-start(bf16[1,128,512]{2,1,0:T(8,128)(2,1)} %param.7) | copy-start | bytes 393220
  58.0 1.1 %copy-start = (f32[1288,128]{1,0:T(8,128)S(1)}, f32[1288,128]{1,0:T(8,128)}, u32[]{:S(2)}) copy-start(f32[1288,128]{1,0:T(8,128)} %shard_map.73.packed_ref) | copy-start | bytes 1978372

commit v4 on v3

--- a/solution.py
+++ b/solution.py
@@ -90,19 +90,25 @@
         )
     work[members : members + cells, :] = anom_ref[...].astype(jnp.float32)
 
-    @pl.loop(0, members // BLK)
-    def _(p):
-        off = pl.multiple_of(p * BLK, BLK)
-        inv = inverse_factor(work[pl.ds(off, BLK), pl.ds(off, BLK)])
+    for off in range(0, members, BLK):
+        end = off + BLK
+        inv = inverse_factor(work[off:end, off:end])
         x = lax.dot_general(
-            work[:, pl.ds(off, BLK)], inv, NT, precision=HI, preferred_element_type=jnp.float32
+            work[end:total, off:end], inv, NT, precision=HI, preferred_element_type=jnp.float32
         )
-        rows = lax.broadcasted_iota(jnp.int32, (total, 1), 0)
-        x = jnp.where(rows >= off + BLK, x, 0.0)
-        work[...] -= lax.dot_general(
-            x, x[:members], NT, precision=HI, preferred_element_type=jnp.float32
-        )
-        work[members:total, pl.ds(off, BLK)] = x[members:]
+        work[members:total, off:end] = x[members - end :]
+        if end < members:
+            work[end : end + BLK, end : end + BLK] -= lax.dot_general(
+                x[:BLK], x[:BLK], NT, precision=HI, preferred_element_type=jnp.float32
+            )
+            work[end + BLK : total, end : end + BLK] -= lax.dot_general(
+                x[BLK:], x[:BLK], NT, precision=HI, preferred_element_type=jnp.float32
+            )
+        for at in range(end + BLK, members, BLK):
+            work[at:total, at : at + BLK] -= lax.dot_general(
+                x[at - end :], x[at - end : at - end + BLK], NT, precision=HI,
+                preferred_element_type=jnp.float32,
+            )
 
     solved = work[members : members + cells, :]
     shift = jnp.sum(solved * work[members + cells : members + cells + 1, :], axis=1, keepdims=True)

time: 84.3 us -> 80.5 us (0.955)
  Pallas kernels: 83 us -> 79.2 us
    pallas_call x1, Pallas kernels: 25.1 us -> 21.2 us  [finish(): pl.pallas_call(finish_kernel, out_shape=jax.ShapeDtypeStruct((ncells, mem...]
where the time goes in v4:
time: 80.5 us; the launch traced here: 80.3 us
  Pallas kernels  79.2 us (98%)
  local copies, waits for them, and re-layouts  1.09 us (1%)
    pallas_call x1, Pallas kernels, observe(): pl.pallas_call(functools.partial(observe_kernel, obs_n, state_n), out_sha...  58 us
    pallas_call x1, Pallas kernels, finish(): pl.pallas_call(finish_kernel, out_shape=jax.ShapeDtypeStruct((ncells, mem...  21.2 us

profile of v4, /device:TPU:0, one launch (start us, length us, event | category | flops | bytes accessed | tf_op | source)
XLA Modules:
  0.0 80.3 jit_solution(11470021399720791012)
XLA Ops:
  0.0 0.0 copy-start.2
  0.0 0.0 copy-start.1
  0.0 58.0 %shard_map.73.packed_ref = f32[1288,128]{1,0:T(8,128)} custom-call(s32[8,8]{1,0:T(8,128)} %bitcast.7, s32[8]{0:T(128)} %counts_ref.1, bf16[128,512]{1,0:T(8,128)(2,1)} %bitcast.4, f32[1,128]{1,0:T(1,128)} %mean_ref.1, bf16[8,8,128,128]{3,2,1,0:T(8,128)(2,1)} %bitcast.6, f32[8,128]{1,0:T(8,128)} %read_hbm.1, f32[8,128]{1,0:T(8,128)} %std_hbm.1), custom_call_target="tpu_custom_call" | custom-call | tf_op jit(solution)/shard_map/pallas_call | solution.py:382
  58.0 0.0 copy-done.2
  58.0 0.0 copy-done.1
  58.0 0.0 copy-start
  58.0 1.1 %copy-done = f32[1288,128]{1,0:T(8,128)S(1)} copy-done((f32[1288,128]{1,0:T(8,128)S(1)}, f32[1288,128]{1,0:T(8,128)}, u32[]{:S(2)}) %copy-start) | copy-done | bytes 659480
  59.1 21.2 %shard_map.74 = bf16[128,512]{1,0:T(8,128)(2,1)} custom-call(f32[1288,128]{1,0:T(8,128)S(1)} %copy-done, bf16[128,512]{1,0:T(8,128)(2,1)S(1)} %bitcast.5, f32[1,128]{1,0:T(1,128)S(1)} %copy-done.2), custom_call_target="tpu_custom_call" | custom-call | tf_op jit(solution)/shard_map/pallas_call | solution.py:122
Async XLA Ops:
  0.0 58.0 %copy-start.2 = (f32[1,128]{1,0:T(1,128)S(1)}, f32[1,128]{1,0:T(1,128)}, u32[]{:S(2)}) copy-start(f32[1,128]{1,0:T(1,128)} %mean_ref.1) | copy-start | bytes 1540
  0.0 58.0 %copy-start.1 = (bf16[1,128,512]{2,1,0:T(8,128)(2,1)S(1)}, bf16[1,128,512]{2,1,0:T(8,128)(2,1)}, u32[]{:S(2)}) copy-start(bf16[1,128,512]{2,1,0:T(8,128)(2,1)} %param.7) | copy-start | bytes 393220
  58.0 1.1 %copy-start = (f32[1288,128]{1,0:T(8,128)S(1)}, f32[1288,128]{1,0:T(8,128)}, u32[]{:S(2)}) copy-start(f32[1288,128]{1,0:T(8,128)} %shard_map.73.packed_ref) | copy-start | bytes 1978372
